TPU v7x, 32 devices: a whole 2x2x4 slice. The times are simulated.
32 devices in a mesh: rep: 4 (over z), fsdp: 8 (over y, x, core).
Axes of the slice: x: 2, y: 2, z: 4, core: 2. Of those that a mesh axis runs over, the one named last changes fastest.
Arguments:
- hidden: bfloat16 [4096, 8192], P(('rep', 'fsdp')), may hold values from -6 to 6
- gain: float32 [8192], replicated, may hold values from 0.1 to 1.9
- key_weight: bfloat16 [4, 8192, 512], P('rep', 'fsdp'), may hold values from -6 to 6
- moment: float32 [4, 8192, 512], P('rep', 'fsdp'), may hold values from -4 to 4
- second: float32 [4, 8192, 512], P('rep', 'fsdp'), may hold values from 0.05 to 1
- dkeys: bfloat16 [4096, 512], P(('rep', 'fsdp')), may hold values from -6 to 6
- step: int32 [], replicated, may hold values from 0 to 29
Outputs:
- keys: bfloat16 [4096, 512], P(('rep', 'fsdp'))
- new_weight: bfloat16 [4, 8192, 512], P('rep', 'fsdp')
- new_moment: float32 [4, 8192, 512], P('rep', 'fsdp')
- new_second: float32 [4, 8192, 512], P('rep', 'fsdp')
All inputs are finite; a program needn't handle non-finite values.
Results may differ from a plain program's by a relative error of at most 0.0051.
Values may be sent and summed in bfloat16 or wider, within the bound.
A program may use at most 64 MiB of HBM per device.

v0:
```python
import math

import jax
import jax.numpy as jnp
from jax import lax
from jax.sharding import PartitionSpec as P

HEAD = 128


def as_sent(x):

    def short(part):
        return part.astype(jnp.bfloat16) if part.dtype == jnp.float32 else part

    return jax.tree.map(short, x)


def from_behind(block, axis, distance):
    devices = range(lax.axis_size(axis))
    route = [((i - distance) % len(devices), i) for i in devices]
    return lax.ppermute(block, axis, route)


def rotate(values, positions, sign):
    count = values.shape[0]
    heads = values.reshape(count, -1, HEAD)
    half = HEAD // 2
    freq = jnp.exp(jnp.arange(half).astype(jnp.float32) * (-2.0 * math.log(500000.0) / HEAD))
    angle = positions.astype(jnp.float32)[:, None] * freq[None, :]
    cosine = jnp.cos(angle)[:, None, :]
    sine = jnp.sin(angle)[:, None, :]
    first = heads[..., :half]
    latter = heads[..., half:]
    turned = jnp.concatenate(
        [first * cosine - sign * latter * sine, latter * cosine + sign * first * sine], axis=-1
    )
    return turned.reshape(count, -1)


def from_partner(values, offset):
    if offset == 0:
        return values
    return jax.tree.map(
        lambda part, own: part.astype(own.dtype),
        from_behind(as_sent(values), "rep", offset),
        values,
    )


def per_device(hidden, gain, key_weight, moment, second, dkeys, step):
    tok_rows = hidden.shape[0]
    width = hidden.shape[1]
    scale = width ** (-0.5)
    weight = key_weight[0]
    values = hidden.astype(jnp.float32)
    inverse = lax.rsqrt(jnp.mean(values * values, axis=-1, keepdims=True) + 1e-05)
    normed = (values * inverse * gain).astype(jnp.bfloat16)
    positions = lax.axis_index("fsdp") * tok_rows + jnp.arange(tok_rows)
    dpre = rotate(dkeys.astype(jnp.float32), positions, -1.0).astype(jnp.bfloat16)
    pre = (
        jnp.dot(
            normed,
            lax.all_gather(weight, "fsdp", axis=0, tiled=True),
            preferred_element_type=jnp.float32,
        )
        * scale
    )
    turned = rotate(pre, positions, 1.0).astype(jnp.bfloat16)
    slices = lax.all_to_all(normed, "fsdp", split_axis=1, concat_axis=0, tiled=True)
    gathered = lax.all_gather(dpre, "fsdp", axis=0, tiled=True)
    total = lax.dot_general(
        slices, gathered, (((0,), (0,)), ((), ())), preferred_element_type=jnp.float32
    )
    grad = total * scale
    count = (step + 1).astype(jnp.float32)
    new_moment = 0.9 * moment[0] + 0.1 * grad
    new_second = 0.95 * second[0] + 0.05 * grad * grad
    mhat = new_moment / (1.0 - jnp.power(jnp.float32(0.9), count))
    vhat = new_second / (1.0 - jnp.power(jnp.float32(0.95), count))
    weight32 = weight.astype(jnp.float32)
    local = (weight32 - 0.05 * (mhat / (jnp.sqrt(vhat) + 1e-08) + 0.1 * weight32)).astype(
        jnp.bfloat16
    )
    groups = lax.axis_size("rep")
    other = lax.switch(
        step % 3,
        [
            lambda values: from_partner(values, 1 % groups),
            lambda values: from_partner(values, 2 % groups),
            lambda values: from_partner(values, 4 % groups),
        ],
        local,
    )
    new_weight = ((local.astype(jnp.float32) + other.astype(jnp.float32)) * 0.5).astype(
        jnp.bfloat16
    )
    return (turned, new_weight[None], new_moment[None], new_second[None])


def solution(mesh):
    return jax.shard_map(
        per_device,
        mesh=mesh,
        in_specs=(
            P(("rep", "fsdp"), None),
            P(),
            P("rep", "fsdp", None),
            P("rep", "fsdp", None),
            P("rep", "fsdp", None),
            P(("rep", "fsdp"), None),
            P(),
        ),
        out_specs=(
            P(("rep", "fsdp"), None),
            P("rep", "fsdp", None),
            P("rep", "fsdp", None),
            P("rep", "fsdp", None),
        ),
        check_vma=False,
    )
```

profile of v0, /device:TPU:1, one launch (start us, length us, event | category | flops | bytes accessed | tf_op | source)
XLA Modules:
  0.0 136.3 jit_solution(9722651964358089922)
XLA Ops:
  7.2 0.0 all-gather.6.cloned.1.call-start
  7.2 0.7 all-gather.6.cloned.1.call-update
  7.9 3.2 %copy.11 = bf16[128,8192]{0,1:T(8,128)(2,1)S(1)} copy(bf16[128,8192]{1,0:T(8,128)(2,1)} %param.10) | data formatting | bytes 4194304 | tf_op args[0]
  11.1 0.0 copy-start.2
  11.1 1.1 fusion.2
  12.3 4.3 %fusion.4 = bf16[128,8192]{0,1:T(8,128)(2,1)} fusion(bf16[128,8192]{0,1:T(8,128)(2,1)S(1)} %copy.11, f32[8192]{0:T(1024)S(1)} %copy-done.2, f32[128]{0:T(128)S(1)} %add_rsqrt_fusion), kind=kLoop, calls=%fused_computation.6 | loop fusion | flops 4194304 | bytes 4227584 | tf_op jit(solution)/shard_map/convert_element_type | solution.py:58
  16.6 5.3 %all-to-all-start = ((bf16[128,8,1024]{0,2,1:T(8,128)(2,1)}), bf16[128,8,1024]{0,2,1:T(8,128)(2,1)S(1)}, u32[]{:S(2)}, u32[]{:S(2)}) async-start(bf16[128,8,1024]{0,2,1:T(8,128)(2,1)} %bitcast.3), calls=%async_computation | async-start | bytes 4194304 | tf_op jit(solution)/shard_map/all_to_all | solution.py:70
  21.9 0.1 reshape.99
  22.1 0.3 broadcast_multiply_fusion
  22.4 65.1 %all-gather.6.cloned.1.call-done = bf16[1,8192,512]{2,1,0:T(8,128)(2,1)} async-done(((bf16[1,1024,512]{2,1,0:T(8,128)(2,1)}), bf16[1,8192,512]{2,1,0:T(8,128)(2,1)}) %all-gather.6.cloned.1.call-update) | async-done | bytes 8388624 | tf_op jit(solution)/shard_map/all_gather | solution.py:64
  87.5 5.3 %fusion.8 = f32[128,512]{1,0:T(8,128)S(1)} fusion(bf16[128,8192]{0,1:T(8,128)(2,1)} %fusion.4, bf16[1,8192,512]{2,1,0:T(8,128)(2,1)} %all-gather.6.cloned.1.call-done), kind=kOutput, calls=%fused_computation.15 | convolution fusion | flops 1073807360 | bytes 10747904 | tf_op jit(solution)/shard_map/dot_general | solution.py:62
  92.8 0.1 reshape.95
  92.9 0.5 subtract_convert_fusion
  93.4 0.4 pad_maximum_fusion
  93.7 0.7 copy.17
  94.4 0.0 all-gather.4.cloned.1.call-update
  95.2 0.0 copy-start
  95.2 2.6 %copy.12 = bf16[8,128,1024]{2,1,0:T(8,128)(2,1)} copy(bf16[8,128,1024]{1,2,0:T(8,128)(2,1)S(1)} %bitcast.40) | data formatting | bytes 4194304 | tf_op jit(solution)/shard_map/all_to_all | solution.py:70
  97.9 0.7 copy.18
  98.5 19.4 %all-gather.4.cloned.1.call-done = bf16[1024,512]{1,0:T(8,128)(2,1)} async-done(((bf16[128,512]{1,0:T(8,128)(2,1)}), bf16[1024,512]{1,0:T(8,128)(2,1)}) %all-gather.4.cloned.1.call-update) | async-done | bytes 1048592 | tf_op jit(solution)/shard_map/all_gather | solution.py:71
  117.9 8.0 %fusion.13 = (f32[1,1024,512]{2,1,0:T(8,128)}, bf16[1024,512]{1,0:T(8,128)(2,1)S(1)}, f32[1,1024,512]{2,1,0:T(8,128)}) fusion(f32[1,1024,512]{2,1,0:T(8,128)} %param.14, f32[]{:T(128)S(6)} %sub.18, f32[]{:T(128)S(6)} %sub.17, f32[1,1024,512]{2,1,0:T(8,128)} %param.13, bf16[1,1024,512]{2,1,0:T(8,128)(2,1)S(1)} %copy-done, bf16[1024,1024]{1,0:T(8,128)(2,1)} %bitcast.41, ...), kind=kOutput, calls=%fused_computation.18 | convolution fusion | flops 1083179008 | bytes 13631496 | tf_op jit(solution)/shard_map/dot_general | solution.py:72
  125.9 1.0 conditional.4
  125.9 1.0 copy.21
  126.9 2.5 %fusion.11 = bf16[1,1024,512]{2,1,0:T(8,128)(2,1)} fusion(bf16[1024,512]{1,0:T(8,128)(2,1)} %get-tuple-element.33, bf16[1024,512]{1,0:T(8,128)(2,1)S(1)} %get-tuple-element.20), kind=kLoop, calls=%fused_computation.16 | loop fusion | flops 2621440 | bytes 3145728 | tf_op jit(solution)/shard_map/broadcast_in_dim | solution.py:98
  (9 shorter events, 0.0 us)
Async XLA Ops:
  7.2 80.3 %all-gather.6.cloned.1.call-start = ((), (), s32[]{:S(2)}) async-start(), calls=%async_computation.2 | async-start | bytes 9437184 | tf_op jit(solution)/shard_map/all_gather | solution.py:64
  11.1 1.1 copy-start.2
  16.6 5.4 %copy-start.1 = (bf16[128,512]{1,0:T(8,128)(2,1)S(1)}, bf16[128,512]{1,0:T(8,128)(2,1)}, u32[]{:S(2)}) copy-start(bf16[128,512]{1,0:T(8,128)(2,1)} %param.15) | copy-start | bytes 393220
  16.6 78.6 %all-to-all-start = ((bf16[128,8,1024]{0,2,1:T(8,128)(2,1)}), bf16[128,8,1024]{0,2,1:T(8,128)(2,1)S(1)}, u32[]{:S(2)}, u32[]{:S(2)}) async-start(bf16[128,8,1024]{0,2,1:T(8,128)(2,1)} %bitcast.3), calls=%async_computation | async-start | bytes 4194304 | tf_op jit(solution)/shard_map/all_to_all | solution.py:70
  21.9 96.0 %all-gather.4.cloned.1.call-start = ((), (), s32[]{:S(2)}) async-start(), calls=%async_computation.1 | async-start | bytes 1179648 | tf_op jit(solution)/shard_map/all_gather | solution.py:71
  95.2 22.7 %copy-start = (bf16[1,1024,512]{2,1,0:T(8,128)(2,1)S(1)}, bf16[1,1024,512]{2,1,0:T(8,128)(2,1)}, u32[]{:S(2)}) copy-start(bf16[1,1024,512]{2,1,0:T(8,128)(2,1)} %param.12) | copy-start | bytes 3145732
Sparse Core Ops, SparseCore 0:
  9.9 77.5 all-gather.5
  94.6 23.3 all-gather.3
where the time goes:
time: 137 us; the launch traced here: 136 us
  waiting for transfers between devices  85.2 us (62%)
  between operations  14.9 us (11%)
  matrix products  13.3 us (10%)
  other arithmetic  9.1 us (7%)
  local copies, waits for them, and re-layouts  8.39 us (6%)
  starting transfers between devices  5.38 us (4%)
    all_gather x1, waiting for transfers between devices, per_device(): lax.all_gather(weight, 'fsdp', axis=0, tiled=True)  65.1 us
    all_gather x1, waiting for transfers between devices, per_device(): gathered = lax.all_gather(dpre, 'fsdp', axis=0, tiled=True)  19.4 us
    dot_general x1, matrix products, per_device(): lax.dot_general(slices, gathered, (((0,), (0,)), ((), ())), preferred_ele...  7.97 us
    all_to_all x1, starting transfers between devices, per_device(): lax.all_to_all(normed, 'fsdp', split_axis=1, concat_axis=0, tiled=True)  5.34 us
    dot_general x1, matrix products, per_device(): jnp.dot(normed, lax.all_gather(weight, 'fsdp', axis=0, tiled=True), prefe...  5.31 us
    unnamed x9, local copies, waits for them, and re-layouts  4.59 us
    convert_element_type x1, other arithmetic, per_device(): normed = (values * inverse * gain).astype(jnp.bfloat16)  4.34 us
  transfers between devices with their start and end apart: 3, of which 2 were waited for; matrix products, arithmetic and copies ran while one was open for 14% of the time, Pallas kernels for 0%

commit v1 on v0

v1 whole, which is shorter than its diff:
```python
import functools
import math

import jax
import jax.numpy as jnp
from jax import lax
from jax.experimental import pallas as pl
from jax.experimental.pallas import tpu as pltpu
from jax.sharding import PartitionSpec as P

HEAD = 128
LANES = 128
CHUNKS = 4
MESH = pl.DeviceIdType.MESH
bf16 = jnp.bfloat16
f32 = jnp.float32


def loop(low, high, body):
    def step(i, carry):
        body(i)
        return carry

    lax.fori_loop(low, high, step, 0)


def kernel(
    n, groups, offset, chunks,
    hidden, dkeys, weight, moment, second, gain, cosine, sine, factors,
    keys_out, weight_out, moment_out, second_out,
    h_v, dk_v, w_v, m_v, s_v, gcol, inv_v, wg_v, slices, e_all, local_v, other_v,
    part, shares, own, keys_v,
    load_sem, h_send, h_recv, e_send, e_recv, f_send, f_recv, p_send, p_recv, g_send, g_recv, out_sem,
):
    tok = h_v.shape[0]
    width = h_v.shape[1]
    feat, kvw = w_v.shape
    fc = feat // chunks
    scale = width ** (-0.5)
    me = lax.axis_index("fsdp")
    rep = lax.axis_index("rep")
    chips = n // 2
    chip = me // 2
    core = me % 2
    sibling = me + 1 - 2 * core

    loads = [
        pltpu.make_async_copy(src, dst, load_sem.at[i])
        for i, (src, dst) in enumerate(
            ((hidden, h_v), (dkeys, dk_v), (weight, w_v), (moment, m_v), (second, s_v))
        )
    ]
    for copy in loads:
        copy.start()

    barrier = pltpu.get_barrier_semaphore()

    def greet(o):
        pl.semaphore_signal(barrier, inc=1, device_id=(rep, (me + o) % n), device_id_type=MESH)

    loop(1, n, greet)
    partners = sorted({offset % groups, (groups - offset) % groups} - {0})
    for distance in partners:
        pl.semaphore_signal(
            barrier, inc=1, device_id=((rep + distance) % groups, me), device_id_type=MESH
        )
    pl.semaphore_wait(barrier, n - 1 + len(partners))

    rows_of = lambda index: pl.ds(pl.multiple_of(index * tok, tok), tok)
    chunk_of = lambda c: pl.ds(pl.multiple_of(c * fc, fc), fc)

    def own_slice(c):
        columns = pl.ds(pl.multiple_of(me * feat + c * fc, LANES), fc)
        return pltpu.make_async_copy(
            hidden.at[:, columns], slices.at[c, rows_of(me)], h_recv.at[c * n]
        )

    def slice_to(c, o):
        peer = (me + o) % n
        columns = pl.ds(pl.multiple_of(peer * feat + c * fc, LANES), fc)
        return pltpu.make_async_remote_copy(
            src_ref=hidden.at[:, columns],
            dst_ref=slices.at[c, rows_of(me)],
            send_sem=h_send.at[c * n + o],
            recv_sem=h_recv.at[c * n + o],
            device_id=(rep, peer),
            device_id_type=MESH,
        )

    def send_chunk(c):
        loop(1, n, lambda o: slice_to(c, o).start())
        own_slice(c).start()

    def wait_chunk(c):
        own_slice(c).wait()
        loop(1, n, lambda o: slice_to(c, o).wait_recv())

    send_chunk(0)

    loads[0].wait()
    block = 16

    def norm(i):
        rows = pl.ds(pl.multiple_of(i * block, block), block)
        values = h_v[rows, :].astype(f32)
        mean = jnp.sum(values * values, axis=-1, keepdims=True) * (1.0 / width)
        inv_v[rows, :] = jnp.broadcast_to(lax.rsqrt(mean + 1e-05), (block, LANES))

    loop(0, tok // block, norm)
    loads[1].wait()
    heads = [slice(i * HEAD, (i + 1) * HEAD) for i in range(kvw // HEAD)]
    for head in heads:
        x = dk_v[:, head].astype(f32)
        turned = x * cosine[...] - pltpu.roll(x, HEAD // 2, 1) * sine[...]
        e_all[rows_of(me), head] = (turned * inv_v[...]).astype(bf16)

    loads[2].wait()
    tiles = feat // LANES
    for i in range(tiles):
        row = gain[pl.ds(me * tiles + i, 1), :]
        rows = slice(i * LANES, (i + 1) * LANES)
        column = jnp.broadcast_to(row, (LANES, LANES)).T
        gcol[rows, :] = column
        for head in heads:
            wg_v[rows, head] = (w_v[rows, head].astype(f32) * column).astype(bf16)

    def e_to(q):
        peer = jnp.where(q == 0, sibling, ((chip + q) % chips) * 2 + core)
        return pltpu.make_async_remote_copy(
            src_ref=e_all.at[rows_of(me)],
            dst_ref=e_all.at[rows_of(me)],
            send_sem=e_send.at[q],
            recv_sem=e_recv.at[q],
            device_id=(rep, peer),
            device_id_type=MESH,
        )

    def forward(q):
        source = ((chip + chips - q) % chips) * 2 + core
        return pltpu.make_async_remote_copy(
            src_ref=e_all.at[rows_of(source)],
            dst_ref=e_all.at[rows_of(source)],
            send_sem=f_send.at[q],
            recv_sem=f_recv.at[q],
            device_id=(rep, sibling),
            device_id_type=MESH,
        )

    loop(1, chips, lambda q: e_to(q).start())
    e_to(0).start()
    loop(1, chunks, send_chunk)

    def relay(q):
        e_to(q).wait_recv()
        forward(q).start()

    loop(1, chips, relay)
    e_to(0).wait_recv()
    loop(1, chips, lambda q: forward(q).wait_recv())
    loads[3].wait()
    loads[4].wait()

    def gossip(c):
        rows = chunk_of(c)
        return pltpu.make_async_remote_copy(
            src_ref=local_v.at[rows],
            dst_ref=other_v.at[rows],
            send_sem=g_send.at[c],
            recv_sem=g_recv.at[c],
            device_id=((rep + offset) % groups, me),
            device_id_type=MESH,
        )

    def out_moment(c):
        return pltpu.make_async_copy(m_v.at[chunk_of(c)], moment_out.at[chunk_of(c)], out_sem.at[c])

    def out_second(c):
        return pltpu.make_async_copy(
            s_v.at[chunk_of(c)], second_out.at[chunk_of(c)], out_sem.at[chunks + c]
        )

    def out_weight(c):
        return pltpu.make_async_copy(
            (other_v if offset else local_v).at[chunk_of(c)],
            weight_out.at[chunk_of(c)],
            out_sem.at[2 * chunks + c],
        )

    def update(c):
        rows = chunk_of(c)
        total = lax.dot_general(
            slices[c], e_all[...], (((0,), (0,)), ((), ())), preferred_element_type=f32
        )
        columns = gcol[rows, :] * scale
        for head in heads:
            grad = total[:, head] * columns
            new_moment = 0.9 * m_v[rows, head] + 0.1 * grad
            new_second = 0.95 * s_v[rows, head] + 0.05 * grad * grad
            m_v[rows, head] = new_moment
            s_v[rows, head] = new_second
            w32 = w_v[rows, head].astype(f32)
            ratio = (new_moment * factors[0]) / (jnp.sqrt(new_second * factors[1]) + 1e-08)
            local_v[rows, head] = (w32 - 0.05 * (ratio + 0.1 * w32)).astype(bf16)
        out_moment(c).start()
        out_second(c).start()
        if offset:
            gossip(c).start()
        else:
            out_weight(c).start()

    def consume(c):
        wait_chunk(c)
        update(c)

    loop(0, chunks - 1, consume)
    wait_chunk(chunks - 1)

    def product(rows):
        total = jnp.zeros((tok, kvw), f32)
        for c in range(chunks):
            total += jnp.dot(
                slices[c, rows, :], wg_v[c * fc : (c + 1) * fc, :], preferred_element_type=f32
            )
        return total

    def share_to(o):
        peer = (me + o) % n
        return pltpu.make_async_remote_copy(
            src_ref=part.at[peer],
            dst_ref=shares.at[me],
            send_sem=p_send.at[o],
            recv_sem=p_recv.at[o],
            device_id=(rep, peer),
            device_id_type=MESH,
        )

    def pre_share(o):
        peer = (me + o) % n
        part[peer] = product(rows_of(peer)).astype(bf16)
        share_to(o).start()

    loop(1, n, pre_share)
    update(chunks - 1)
    own[...] = product(rows_of(me))

    def add_share(o):
        share_to(o).wait_recv()
        own[...] += shares[(me + n - o) % n].astype(f32)

    loop(1, n, add_share)
    for head in heads:
        x = own[:, head] * inv_v[...] * scale
        keys_v[:, head] = (
            x * cosine[...] + pltpu.roll(x, HEAD // 2, 1) * sine[...]
        ).astype(bf16)
    keys_copy = pltpu.make_async_copy(keys_v, keys_out, out_sem.at[3 * chunks])
    keys_copy.start()

    if offset:

        def mix(c):
            gossip(c).wait()
            rows = chunk_of(c)
            mean = (local_v[rows, :].astype(f32) + other_v[rows, :].astype(f32)) * 0.5
            other_v[rows, :] = mean.astype(bf16)
            out_weight(c).start()

        loop(0, chunks, mix)

    def drain(c):
        loop(1, n, lambda o: slice_to(c, o).wait_send())
        out_moment(c).wait()
        out_second(c).wait()
        out_weight(c).wait()

    loop(0, chunks, drain)
    loop(0, chips, lambda q: e_to(q).wait_send())
    loop(1, chips, lambda q: forward(q).wait_send())
    loop(1, n, lambda o: share_to(o).wait_send())
    keys_copy.wait()


def fused(offset, ident, n, groups, operands):
    hidden, dkeys, weight = operands[:3]
    tok, width = hidden.shape
    feat, kvw = weight.shape
    chunks = CHUNKS if feat % (CHUNKS * LANES) == 0 else max(1, feat // LANES)
    fc = feat // chunks
    chips = n // 2
    anywhere = pl.BlockSpec(memory_space=pl.ANY)
    vmem = pl.BlockSpec(memory_space=pltpu.VMEM)
    dma = pltpu.SemaphoreType.DMA
    return pl.pallas_call(
        functools.partial(kernel, n, groups, offset, chunks),
        out_shape=(
            jax.ShapeDtypeStruct((tok, kvw), bf16),
            jax.ShapeDtypeStruct((feat, kvw), bf16),
            jax.ShapeDtypeStruct((feat, kvw), f32),
            jax.ShapeDtypeStruct((feat, kvw), f32),
        ),
        in_specs=[anywhere] * 5 + [vmem] * 3 + [pl.BlockSpec(memory_space=pltpu.SMEM)],
        out_specs=(anywhere,) * 4,
        scratch_shapes=[
            pltpu.VMEM((tok, width), bf16),
            pltpu.VMEM((tok, kvw), bf16),
            pltpu.VMEM((feat, kvw), bf16),
            pltpu.VMEM((feat, kvw), f32),
            pltpu.VMEM((feat, kvw), f32),
            pltpu.VMEM((feat, LANES), f32),
            pltpu.VMEM((tok, LANES), f32),
            pltpu.VMEM((feat, kvw), bf16),
            pltpu.VMEM((chunks, n * tok, fc), bf16),
            pltpu.VMEM((n * tok, kvw), bf16),
            pltpu.VMEM((feat, kvw), bf16),
            pltpu.VMEM((feat, kvw), bf16),
            pltpu.VMEM((n, tok, kvw), bf16),
            pltpu.VMEM((n, tok, kvw), bf16),
            pltpu.VMEM((tok, kvw), f32),
            pltpu.VMEM((tok, kvw), bf16),
            dma((5,)),
            dma((chunks * n,)),
            dma((chunks * n,)),
            dma((chips,)),
            dma((chips,)),
            dma((chips,)),
            dma((chips,)),
            dma((n,)),
            dma((n,)),
            dma((chunks,)),
            dma((chunks,)),
            dma((3 * chunks + 1,)),
        ],
        compiler_params=pltpu.CompilerParams(
            collective_id=ident, has_side_effects=True, vmem_limit_bytes=60 * 2**20
        ),
    )(*operands)


def per_device(hidden, gain, key_weight, moment, second, dkeys, step):
    tok_rows, width = hidden.shape
    n = lax.axis_size("fsdp")
    groups = lax.axis_size("rep")
    positions = lax.axis_index("fsdp") * tok_rows + jnp.arange(tok_rows)
    half = HEAD // 2
    freq = jnp.exp(jnp.arange(half).astype(f32) * (-2.0 * math.log(500000.0) / HEAD))
    angle = positions.astype(f32)[:, None] * freq[None, :]
    cos, sin = jnp.cos(angle), jnp.sin(angle)
    cosine = jnp.concatenate([cos, cos], axis=-1)
    sine = jnp.concatenate([-sin, sin], axis=-1)
    count = (step + 1).astype(f32)
    factors = jnp.stack(
        [1.0 / (1.0 - jnp.power(f32(0.9), count)), 1.0 / (1.0 - jnp.power(f32(0.95), count))]
    )
    operands = (
        hidden, dkeys, key_weight[0], moment[0], second[0],
        gain.reshape(-1, LANES), cosine, sine, factors,
    )
    branches = [
        functools.partial(lambda d, i, *ops: fused(d % groups, i, n, groups, ops), d, i)
        for i, d in enumerate((1, 2, 4))
    ]
    keys, new_weight, new_moment, new_second = lax.switch(step % 3, branches, *operands)
    return (keys, new_weight[None], new_moment[None], new_second[None])


def solution(mesh):
    return jax.shard_map(
        per_device,
        mesh=mesh,
        in_specs=(
            P(("rep", "fsdp"), None),
            P(),
            P("rep", "fsdp", None),
            P("rep", "fsdp", None),
            P("rep", "fsdp", None),
            P(("rep", "fsdp"), None),
            P(),
        ),
        out_specs=(
            P(("rep", "fsdp"), None),
            P("rep", "fsdp", None),
            P("rep", "fsdp", None),
            P("rep", "fsdp", None),
        ),
        check_vma=False,
    )
```

time: 137 us -> 59.3 us (0.43)
  waiting for transfers between devices: 85.2 us -> 0 us
  Pallas kernels: 0 us -> 51.7 us
  between operations: 14.9 us -> 1.49 us
  matrix products: 13.3 us -> 0 us
  other arithmetic: 9.1 us -> 0.5 us
  starting transfers between devices: 5.38 us -> 0 us
  local copies, waits for them, and re-layouts: 8.39 us -> 5.29 us
    all_gather x2 -> x0, waiting for transfers between devices: 84.5 us -> none  [the longest x1 65.1 us: per_device(): lax.all_gather(weight, 'fsdp', axis=0, tiled=True)]
    pallas_call x0 -> x1, Pallas kernels: none -> 51.7 us  [fused(): pl.pallas_call(functools.partial(kernel, n, groups, offset, chunks), out_...]
    dot_general x2 -> x0, matrix products: 13.3 us -> none  [the longest x1 7.97 us: per_device(): lax.dot_general(slices, gathered, (((0,), (0,)), ((), ())), preferred_ele...]
    all_to_all x1 -> x0, starting transfers between devices: 5.34 us -> none  [per_device(): lax.all_to_all(normed, 'fsdp', split_axis=1, concat_axis=0, tiled=True)]
    convert_element_type x2 -> x1, other arithmetic: 4.35 us -> 0.01 us  [per_device(): angle = positions.astype(f32)[:, None] * freq[None, :]]
    all_to_all x1 -> x0, local copies, waits for them, and re-layouts: 2.64 us -> none  [per_device(): lax.all_to_all(normed, 'fsdp', split_axis=1, concat_axis=0, tiled=True)]
    broadcast_in_dim x1 -> x0, other arithmetic: 2.52 us -> none  [per_device(): return (turned, new_weight[None], new_moment[None], new_second[None])]
    unnamed x9 -> x6, local copies, waits for them, and re-layouts: 4.59 us -> 5.29 us
  transfers between devices with their start and end apart: 3 -> 0, of which waited for: 2 -> 0; matrix products, arithmetic and copies ran while one was open for 14% -> 0% of each run, Pallas kernels for 0% -> 0%
where the time goes in v1:
time: 59.3 us; the launch traced here: 59.1 us
  Pallas kernels  51.7 us (87%)
  local copies, waits for them, and re-layouts  5.29 us (9%)
  between operations  1.49 us (3%)
    pallas_call x1, Pallas kernels, fused(): pl.pallas_call(functools.partial(kernel, n, groups, offset, chunks), out_...  51.7 us
    unnamed x6, local copies, waits for them, and re-layouts  5.29 us

profile of v1, /device:TPU:1, one launch (start us, length us, event | category | flops | bytes accessed | tf_op | source)
XLA Modules:
  0.0 59.1 jit_solution(649340307824965333)
XLA Ops:
  1.5 0.1 pad_maximum_fusion.2
  1.5 0.3 fusion
  1.9 0.1 pad_maximum_fusion
  2.0 51.8 %conditional.1 = ((bf16[128,512]{1,0:T(8,128)(2,1)S(1)}, bf16[1024,512]{1,0:T(8,128)(2,1)S(1)}, f32[1024,512]{1,0:T(8,128)S(1)}, f32[1024,512]{1,0:T(8,128)})) conditional(s32[]{:T(128)} %clamp.3, (bf16[128,8192]{1,0:T(8,128)(2,1)}, bf16[128,512]{1,0:T(8,128)(2,1)}, bf16[1024,512]{1,0:T(8,128)(2,1)}, f32[1024,512]{1,0:T(8,128)}, ...), branch_computations={%region_0.1_spmd, %region_1.2_spmd, %region_2.3_spmd} | conditional | bytes 8 | solution.py:362
  2.0 51.7 %branch_0_fun.1 = (bf16[128,512]{1,0:T(8,128)(2,1)S(1)}, bf16[1024,512]{1,0:T(8,128)(2,1)S(1)}, f32[1024,512]{1,0:T(8,128)S(1)}, f32[1024,512]{1,0:T(8,128)}) custom-call(bf16[128,8192]{1,0:T(8,128)(2,1)} %get-tuple-element.69.hidden, bf16[128,512]{1,0:T(8,128)(2,1)} %get-tuple-element.70.dkeys, bf16[1024,512]{1,0:T(8,128)(2,1)} %get-tuple-element.71.weight, ...), custom_call_target="tpu_custom_call" | custom-call | tf_op jit(solution)/shard_map/cond/branch_0_fun/pallas_call | solution.py:293
  53.8 0.7 %copy.28 = bf16[128,512]{1,0:T(8,128)(2,1)} copy(bf16[128,512]{1,0:T(8,128)(2,1)S(1)} %get-tuple-element.141) | data formatting | bytes 262144
  54.4 1.0 %copy.29 = bf16[1,1024,512]{2,1,0:T(8,128)(2,1)} copy(bf16[1,1024,512]{2,1,0:T(8,128)(2,1)S(1)} %bitcast.20) | data formatting | bytes 2097152
  55.4 0.0 copy-start
  55.4 1.3 %copy.30 = f32[1,1024,512]{2,1,0:T(8,128)} copy(f32[1,1024,512]{2,1,0:T(8,128)S(1)} %bitcast.18) | data formatting | bytes 4194304
  56.7 1.0 %copy-done = f32[1024,512]{1,0:T(8,128)S(1)} copy-done((f32[1024,512]{1,0:T(8,128)S(1)}, f32[1024,512]{1,0:T(8,128)}, u32[]{:S(2)}) %copy-start) | copy-done | bytes 2097176
  57.7 1.3 %copy.31 = f32[1,1024,512]{2,1,0:T(8,128)} copy(f32[1,1024,512]{2,1,0:T(8,128)S(1)} %bitcast.19) | data formatting | bytes 4194304
  (2 shorter events, 0.0 us)
Async XLA Ops:
  55.4 2.3 %copy-start = (f32[1024,512]{1,0:T(8,128)S(1)}, f32[1024,512]{1,0:T(8,128)}, u32[]{:S(2)}) copy-start(f32[1024,512]{1,0:T(8,128)} %get-tuple-element.113) | copy-start | bytes 6291460
